TPU v7x, 32 devices: a whole 2x2x4 slice. The times are simulated.
32 devices in a mesh: row: 4 (over y, core), col: 8 (over z, x).
Axes of the slice: x: 2, y: 2, z: 4, core: 2. Of those that a mesh axis runs over, the one named last changes fastest.
Arguments:
- spectra: float32 [2, 16, 1024, 512], P(None, None, ('col', 'row')), as said below
- pair_mask: int32 [4, 8], P('row', 'col'), may hold values 0 or 1
- band_range: int32 [2], replicated, may hold values from 0 to 512, as said below
Outputs:
- correlations: bfloat16 [1024, 1024, 201], P('row', 'col')
Inputs may be any that keep to these rules, and one draw needn't show every extreme that they name: `spectra`: every channel's spectrum carries its own amplitude. band_range[0] < band_range[1].
All inputs are finite; a program needn't handle non-finite values. No bound on the sum of `pair_mask` on one device may be relied on, other than what follows from the above.
Results may differ from a plain program's by a relative error of at most 0.0061.
Values may be sent and summed in bfloat16 or wider, within the bound.
No kernel may reach another device: no remote copies, remote signals or barrier semaphores. Data moves between devices by JAX's collectives and lax.ppermute only.
A program may use at most 320 MiB of HBM per device.

v0:
```python
import math
import jax
import jax.numpy as jnp
from jax import lax
from jax.sharding import PartitionSpec as P

W = 16
FB = 512
LAGS = 201
NFFT = 15000
F0 = 60
EPS = 1e-06


def whiten(spectra):
    power_mean = jnp.mean(spectra[0] * spectra[0] + spectra[1] * spectra[1], axis=-1, keepdims=True)
    return (spectra * lax.rsqrt(power_mean + EPS)).astype(jnp.bfloat16)


def make_table(band_range):
    freq_index = jnp.arange(FB, dtype=jnp.int32)
    lag_index = jnp.arange(LAGS, dtype=jnp.int32) - LAGS // 2
    turns = jnp.mod((F0 + freq_index)[:, None] * lag_index[None, :], NFFT)
    theta = turns.astype(jnp.float32) * (2.0 * math.pi / NFFT)
    inband = ((freq_index >= band_range[0]) & (freq_index < band_range[1])).astype(jnp.float32)[
        :, None
    ]
    return jnp.concatenate([inband * jnp.cos(theta), -inband * jnp.sin(theta)], axis=0).astype(
        jnp.bfloat16
    )


def pair_block(row_block, col_block, lag_table):
    real_part = jnp.einsum(
        "wap,wbp->abp", row_block[0], col_block[0], preferred_element_type=jnp.float32
    ) + jnp.einsum("wap,wbp->abp", row_block[1], col_block[1], preferred_element_type=jnp.float32)
    imag_part = jnp.einsum(
        "wap,wbp->abp", row_block[1], col_block[0], preferred_element_type=jnp.float32
    ) - jnp.einsum("wap,wbp->abp", row_block[0], col_block[1], preferred_element_type=jnp.float32)
    cross = jnp.stack([real_part, imag_part], axis=2).astype(jnp.bfloat16)
    height = row_block.shape[2]
    width = col_block.shape[2]
    flat = cross.reshape(height * width, 2 * FB)
    summed = jnp.dot(flat, lag_table, preferred_element_type=jnp.float32)
    return (summed * (1.0 / math.sqrt(W * FB))).astype(jnp.bfloat16).reshape(height, width, LAGS)


def body(spectra, pair_mask, band_range):
    whitened = whiten(spectra)
    col_block = lax.all_gather(whitened, "row", axis=2, tiled=True)
    block_width = col_block.shape[2]
    row_count = lax.axis_size("row")
    blocks_per_row = lax.axis_size("col") // row_count
    row_id = lax.axis_index("row")
    col_id = lax.axis_index("col")
    shard_width = whitened.shape[2]
    windows = whitened.shape[1]
    bins = whitened.shape[3]
    strided = lax.all_gather(whitened, "col", axis=2, tiled=True)
    grouped = strided.reshape(2, windows, row_count, blocks_per_row, shard_width, bins)
    moved = lax.all_to_all(grouped, "row", split_axis=2, concat_axis=4, tiled=True)
    row_block = moved.reshape(2, windows, blocks_per_row * row_count * shard_width, bins)
    lag_table = make_table(band_range)
    request = (pair_mask[0, 0] == 1) & (col_id >= row_id * blocks_per_row)
    height = row_block.shape[2]
    return lax.cond(
        request,
        lambda: pair_block(row_block, col_block, lag_table),
        lambda: jnp.zeros((height, block_width, LAGS), jnp.bfloat16),
    )


def solution(mesh):
    return jax.shard_map(
        body,
        mesh=mesh,
        in_specs=(P(None, None, ("col", "row"), None), P("row", "col"), P()),
        out_specs=P("row", "col", None),
        check_vma=False,
    )
```

profile of v0, /device:TPU:0, one launch (start us, length us, event | category | flops | bytes accessed | tf_op | source)
XLA Modules:
  0.0 639.6 jit_solution(6515462427543158156)
XLA Ops:
  6.5 0.0 all-gather.5.cloned.1.call-start
  6.5 1.7 add_reduce_fusion
  8.3 2.8 multiply_convert_fusion
  11.1 0.0 all-gather.5.cloned.1.call-update
  11.2 0.0 all-gather.3.cloned.1.call-start
  11.2 0.7 all-gather.3.cloned.1.call-update
  11.9 127.0 %all-gather.5.cloned.1.call-done = bf16[2,16,256,512]{3,2,1,0:T(8,128)(2,1)} async-done(((bf16[2,16,32,512]{3,2,1,0:T(8,128)(2,1)}), bf16[2,16,256,512]{3,2,1,0:T(8,128)(2,1)}) %all-gather.5.cloned.1.call-update) | async-done | bytes 8388624 | tf_op jit(solution)/shard_map/all_gather | solution.py:59
  138.9 9.1 %copy.19 = bf16[2,16,4,2,32,512]{5,4,3,1,0,2:T(8,128)(2,1)} copy(bf16[2,16,4,2,32,512]{5,4,3,2,1,0:T(8,128)(2,1)} %bitcast.59) | data formatting | bytes 16777216 | tf_op jit(solution)/shard_map/reshape | solution.py:60
  148.0 0.0 copy-start.1
  148.0 5.8 all-to-all-start
  154.4 0.0 copy-done.1
  154.4 0.6 fusion.22
  155.0 1.1 fusion.20
  156.1 1.1 fusion.19
  157.3 2.6 multiply_convert_fusion.2
  159.9 0.9 pad_maximum_fusion.1
  160.8 27.1 %all-gather.3.cloned.1.call-done = bf16[2,16,128,512]{3,2,1,0:T(8,128)(2,1)} async-done(((bf16[2,16,32,512]{3,2,1,0:T(8,128)(2,1)}), bf16[2,16,128,512]{3,2,1,0:T(8,128)(2,1)}) %all-gather.3.cloned.1.call-update) | async-done | bytes 4194320 | tf_op jit(solution)/shard_map/all_gather | solution.py:50
  187.9 73.7 %all-to-all-done = bf16[2,16,4,2,32,512]{5,4,3,1,0,2:T(8,128)(2,1)} async-done(((bf16[2,16,4,2,32,512]{5,4,3,1,0,2:T(8,128)(2,1)}), bf16[2,16,4,2,32,512]{5,4,3,1,0,2:T(8,128)(2,1)}, u32[]{:S(2)}, u32[]{:S(2)}) %all-to-all-start) | async-done | bytes 8388640 | tf_op jit(solution)/shard_map/all_to_all | solution.py:61
  261.6 371.2 %conditional.1 = (bf16[256,128,201]{1,0,2:T(8,128)(2,1)}) conditional(s32[]{:T(128)} %convert_element_type.30, () %tuple.11, (bf16[2,16,128,512]{3,2,1,0:T(8,128)(2,1)}, bf16[2,16,1,2,4,32,512]{6,5,3,1,0,4,2:T(8,128)(2,1)}, bf16[1024,201]{1,0:T(8,128)(2,1)}) %tuple.12), branch_computations={%region_1.2_spmd, %region_2.3_spmd} | conditional | flops 15750201344 | bytes 807036928 | solution.py:66
  261.6 7.9 %copy.20 = bf16[2,16,128,512]{2,1,3,0:T(8,128)(2,1)} copy(bf16[2,16,128,512]{3,2,1,0:T(8,128)(2,1)} %get-tuple-element.22) | data formatting | bytes 8388608 | tf_op jit(solution)/shard_map
  269.4 6.2 fusion.21
  275.7 7.9 %copy.14 = bf16[16,256,512]{1,0,2:T(8,128)(2,1)} copy(bf16[16,256,512]{2,1,0:T(8,128)(2,1)} %bitcast.57) | data formatting | bytes 8388608 | tf_op jit(solution)/shard_map/cond/branch_1_fun/squeeze | solution.py:35
  283.6 7.8 %copy.15 = bf16[16,256,512]{1,0,2:T(8,128)(2,1)} copy(bf16[16,256,512]{2,1,0:T(8,128)(2,1)} %bitcast.56) | data formatting | bytes 8388608 | tf_op jit(solution)/shard_map/cond/branch_1_fun/squeeze | solution.py:36
  291.4 26.3 %fusion.11 = f32[512,128,256]{2,1,0:T(8,128)} fusion(bf16[16,256,512]{1,0,2:T(8,128)(2,1)} %copy.15, bf16[2,16,128,512]{2,1,3,0:T(8,128)(2,1)} %copy.20), kind=kOutput, calls=%fused_computation.13 | convolution fusion | flops 536870912 | bytes 73400320 | tf_op jit(solution)/shard_map/cond/branch_1_fun/wap,wbp->abp/dot_general | solution.py:37
  317.7 36.4 %fusion.10 = bf16[256,128,1,512]{0,1,3,2:T(8,128)(2,1)} fusion(f32[512,128,256]{2,1,0:T(8,128)} %fusion.11, bf16[16,256,512]{1,0,2:T(8,128)(2,1)} %copy.14, bf16[2,16,128,512]{2,1,3,0:T(8,128)(2,1)} %copy.20), kind=kOutput, calls=%fused_computation.9 | convolution fusion | flops 570425344 | bytes 106954752 | tf_op jit(solution)/shard_map/cond/branch_1_fun/wap,wbp->abp/dot_general | solution.py:39
  354.1 26.3 %fusion.12 = f32[512,128,256]{2,1,0:T(8,128)} fusion(bf16[16,256,512]{1,0,2:T(8,128)(2,1)} %copy.14, bf16[2,16,128,512]{2,1,3,0:T(8,128)(2,1)} %copy.20), kind=kOutput, calls=%fused_computation.14 | convolution fusion | flops 536870912 | bytes 73400320 | tf_op jit(solution)/shard_map/cond/branch_1_fun/wap,wbp->abp/dot_general | solution.py:34
  380.4 36.3 %fusion.9 = bf16[256,128,1,512]{0,1,3,2:T(8,128)(2,1)} fusion(f32[512,128,256]{2,1,0:T(8,128)} %fusion.12, bf16[16,256,512]{1,0,2:T(8,128)(2,1)} %copy.15, bf16[2,16,128,512]{2,1,3,0:T(8,128)(2,1)} %copy.20), kind=kOutput, calls=%fused_computation.8 | convolution fusion | flops 570425344 | bytes 106954752 | tf_op jit(solution)/shard_map/cond/branch_1_fun/wap,wbp->abp/dot_general | solution.py:36
  416.7 44.6 %pad_maximum_fusion = bf16[256,128,2,512]{0,1,3,2:T(8,128)(2,1)} fusion(bf16[256,128,1,512]{0,1,3,2:T(8,128)(2,1)} %fusion.10, bf16[256,128,1,512]{0,1,3,2:T(8,128)(2,1)} %fusion.9), kind=kLoop, calls=%fused_computation.3 | loop fusion | flops 33554432 | bytes 134217728 | tf_op jit(solution)/shard_map/cond/branch_1_fun/stack | solution.py:40
  461.3 0.0 copy-start
  461.3 81.5 %copy.18 = bf16[256,128,2,512]{1,0,3,2:T(8,128)(2,1)} copy(bf16[256,128,2,512]{0,1,3,2:T(8,128)(2,1)} %pad_maximum_fusion) | data formatting | bytes 134217728 | tf_op jit(solution)/shard_map/cond/branch_1_fun/stack | solution.py:40
  542.8 0.0 copy-done
  542.8 75.7 %fusion.6 = bf16[32768,201]{0,1:T(8,128)(2,1)} fusion(bf16[1024,201]{1,0:T(8,128)(2,1)S(1)} %copy-done, bf16[128,8,256,128]{3,2,1,0:T(8,128)(2,1)} %bitcast.19), kind=kOutput, calls=%fused_computation.7 | convolution fusion | flops 13502054400 | bytes 80693248 | tf_op jit(solution)/shard_map/cond/branch_1_fun/dot_general | solution.py:44
  618.5 8.4 %copy.23 = bf16[26,8,256,128]{3,2,1,0:T(8,128)(2,1)S(1)} copy(bf16[26,8,256,128]{3,1,2,0:T(8,128)(2,1)} %bitcast.58) | data formatting | bytes 27262976 | tf_op jit(solution)/shard_map/cond
  626.8 6.0 slice_bitcast_fusion
  (3 shorter events, 0.0 us)
Async XLA Ops:
  6.5 132.4 %all-gather.5.cloned.1.call-start = ((), (), s32[]{:S(2)}) async-start(), calls=%async_computation.2 | async-start | bytes 9437184 | tf_op jit(solution)/shard_map/all_gather | solution.py:59
  11.2 176.7 %all-gather.3.cloned.1.call-start = ((), (), s32[]{:S(2)}) async-start(), calls=%async_computation.1 | async-start | bytes 5242880 | tf_op jit(solution)/shard_map/all_gather | solution.py:50
  148.0 6.4 %copy-start.1 = (s32[2]{0:T(128)S(1)}, s32[2]{0:T(128)}, u32[]{:S(2)}) copy-start(s32[2]{0:T(128)} %param.7) | copy-start | bytes 28
  148.0 113.6 %all-to-all-start = ((bf16[2,16,4,2,32,512]{5,4,3,1,0,2:T(8,128)(2,1)}), bf16[2,16,4,2,32,512]{5,4,3,1,0,2:T(8,128)(2,1)}, u32[]{:S(2)}, u32[]{:S(2)}) async-start(bf16[2,16,4,2,32,512]{5,4,3,1,0,2:T(8,128)(2,1)} %copy.19), calls=%async_computation | async-start | bytes 16777216 | tf_op jit(solution)/shard_map/all_to_all | solution.py:61
  461.3 81.5 %copy-start = (bf16[1024,201]{1,0:T(8,128)(2,1)S(1)}, bf16[1024,201]{1,0:T(8,128)(2,1)}, u32[]{:S(2)}) copy-start(bf16[1024,201]{1,0:T(8,128)(2,1)} %get-tuple-element.17) | copy-start | bytes 1234948 | tf_op jit(solution)/shard_map/cond
Sparse Core Ops, SparseCore 0:
  11.3 127.5 all-gather.4
  140.5 47.3 all-gather.2
where the time goes:
time: 643 us; the launch traced here: 640 us
  waiting for transfers between devices  229 us (36%)
  matrix products  201 us (31%)
  local copies, waits for them, and re-layouts  135 us (21%)
  other arithmetic  55 us (9%)
  between operations  14.1 us (2%)
    all_gather x1, waiting for transfers between devices, body(): strided = lax.all_gather(whitened, 'col', axis=2, tiled=True)  127 us
    another operation x1, local copies, waits for them, and re-layouts, pair_block(): cross = jnp.stack([real_part, imag_part], axis=2).astype(jnp.bfloat16)  81.5 us
    dot_general x1, matrix products, pair_block(): summed = jnp.dot(flat, lag_table, preferred_element_type=jnp.float32)  75.7 us
    all_to_all x1, waiting for transfers between devices, body(): lax.all_to_all(grouped, 'row', split_axis=2, concat_axis=4, tiled=True)  73.7 us
    another operation x1, other arithmetic, pair_block(): cross = jnp.stack([real_part, imag_part], axis=2).astype(jnp.bfloat16)  44.6 us
    dot_general x1, matrix products, pair_block(): jnp.einsum('wap,wbp->abp', row_block[0], col_block[1], preferred_element_...  36.4 us
    dot_general x1, matrix products, pair_block(): jnp.einsum('wap,wbp->abp', row_block[1], col_block[1], preferred_element_...  36.3 us
    all_gather x1, waiting for transfers between devices, body(): col_block = lax.all_gather(whitened, 'row', axis=2, tiled=True)  27.1 us
  transfers between devices with their start and end apart: 3, of which 3 were waited for; matrix products, arithmetic and copies ran while one was open for 2% of the time, Pallas kernels for 0%

commit v1 on v0

--- a/solution.py
+++ b/solution.py
@@ -47,7 +47,12 @@
 
 def body(spectra, pair_mask, band_range):
     whitened = whiten(spectra)
-    col_block = lax.all_gather(whitened, "row", axis=2, tiled=True)
+    ring = [whitened]
+    for hop in range(3):
+        ring.append(lax.ppermute(ring[-1], "row", [(dev, (dev + 1) % 4) for dev in range(4)]))
+    col_block = jnp.roll(
+        jnp.concatenate(ring[::-1], axis=2), (lax.axis_index("row") + 1) * ring[0].shape[2], axis=2
+    )
     block_width = col_block.shape[2]
     row_count = lax.axis_size("row")
     blocks_per_row = lax.axis_size("col") // row_count

time: 643 us -> 695 us (1.081)
  waiting for transfers between devices: 229 us -> 253 us
  local copies, waits for them, and re-layouts: 135 us -> 155 us
    ppermute x0 -> x3, waiting for transfers between devices: none -> 125 us  [body(): lax.ppermute(ring[-1], 'row', [(dev, (dev + 1) % 4) for dev in range(4)])]
    all_to_all x1, waiting for transfers between devices: 73.7 us -> 0.01 us  [body(): lax.all_to_all(grouped, 'row', split_axis=2, concat_axis=4, tiled=True)]
    all_gather x1 -> x0, waiting for transfers between devices: 27.1 us -> none  [body(): col_block = lax.all_gather(whitened, 'row', axis=2, tiled=True)]
    unnamed x2 -> x16, local copies, waits for them, and re-layouts: 0.01 us -> 13.8 us
  transfers between devices with their start and end apart: 3 -> 5, of which waited for: 3 -> 4; matrix products, arithmetic and copies ran while one was open for 2% -> 3% of each run, Pallas kernels for 0% -> 0%
where the time goes in v1:
time: 695 us; the launch traced here: 692 us
  waiting for transfers between devices  253 us (36%)
  matrix products  206 us (30%)
  local copies, waits for them, and re-layouts  155 us (22%)
  other arithmetic  57.8 us (8%)
  between operations  14.1 us (2%)
    all_gather x1, waiting for transfers between devices, body(): strided = lax.all_gather(whitened, 'col', axis=2, tiled=True)  128 us
    ppermute x3, waiting for transfers between devices, body(): lax.ppermute(ring[-1], 'row', [(dev, (dev + 1) % 4) for dev in range(4)])  125 us
    another operation x1, local copies, waits for them, and re-layouts, pair_block(): cross = jnp.stack([real_part, imag_part], axis=2).astype(jnp.bfloat16)  81.4 us
    dot_general x1, matrix products, pair_block(): summed = jnp.dot(flat, lag_table, preferred_element_type=jnp.float32)  75.6 us
    another operation x1, other arithmetic, pair_block(): cross = jnp.stack([real_part, imag_part], axis=2).astype(jnp.bfloat16)  44.7 us
    dot_general x1, matrix products, pair_block(): jnp.einsum('wap,wbp->abp', row_block[0], col_block[1], preferred_element_...  37.7 us
    dot_general x1, matrix products, pair_block(): jnp.einsum('wap,wbp->abp', row_block[1], col_block[1], preferred_element_...  37.7 us
    dot_general x1, matrix products, pair_block(): jnp.einsum('wap,wbp->abp', row_block[0], col_block[0], preferred_element_...  27.3 us
  transfers between devices with their start and end apart: 5, of which 4 were waited for; matrix products, arithmetic and copies ran while one was open for 3% of the time, Pallas kernels for 0%

profile of v1, /device:TPU:0, one launch (start us, length us, event | category | flops | bytes accessed | tf_op | source)
XLA Modules:
  0.0 692.1 jit_solution(13538995196087253988)
XLA Ops:
  6.5 0.0 all-gather.2.cloned.1.call-start
  6.5 1.7 add_reduce_fusion
  8.3 2.8 multiply_convert_fusion
  11.1 0.0 all-gather.2.cloned.1.call-update
  11.2 127.8 %all-gather.2.cloned.1.call-done = bf16[2,16,256,512]{3,2,1,0:T(8,128)(2,1)} async-done(((bf16[2,16,32,512]{3,2,1,0:T(8,128)(2,1)}), bf16[2,16,256,512]{3,2,1,0:T(8,128)(2,1)}) %all-gather.2.cloned.1.call-update) | async-done | bytes 8388624 | tf_op jit(solution)/shard_map/all_gather | solution.py:64
  138.9 8.4 %copy.20 = bf16[2,16,4,2,32,512]{5,4,3,1,0,2:T(8,128)(2,1)} copy(bf16[2,16,4,2,32,512]{5,4,3,2,1,0:T(8,128)(2,1)} %bitcast.59) | data formatting | bytes 16777216 | tf_op jit(solution)/shard_map/reshape | solution.py:65
  147.4 0.0 copy-start.1
  147.4 0.0 copy-start.5
  147.4 0.0 copy-start
  147.4 5.9 all-to-all-start
  153.3 0.0 copy-done.1
  153.3 0.5 collective-permute-start
  153.8 103.8 %collective-permute-done = bf16[2,16,32,512]{3,2,1,0:T(8,128)(2,1)S(1)} collective-permute-done((bf16[2,16,32,512]{3,2,1,0:T(8,128)(2,1)S(1)}, bf16[2,16,32,512]{3,2,1,0:T(8,128)(2,1)S(1)}, u32[]{:S(2)}, u32[]{:S(2)}) %collective-permute-start) | collective-permute-done | bytes 1048608 | tf_op jit(solution)/shard_map/ppermute | solution.py:52
  257.6 0.0 copy-start.2
  257.6 1.0 copy-done.2
  258.6 0.0 collective-permute-start.1
  258.6 0.0 copy-start.3
  258.6 14.3 %collective-permute-done.1 = bf16[2,16,32,512]{3,2,1,0:T(8,128)(2,1)} collective-permute-done((bf16[2,16,32,512]{3,2,1,0:T(8,128)(2,1)S(1)}, bf16[2,16,32,512]{3,2,1,0:T(8,128)(2,1)}, u32[]{:S(2)}, u32[]{:S(2)}) %collective-permute-start.1) | collective-permute-done | bytes 1048608 | tf_op jit(solution)/shard_map/ppermute | solution.py:52
  272.9 0.0 collective-permute-start.2
  273.6 0.0 copy-done.5
  273.6 0.6 fusion.26
  274.2 1.3 fusion.24
  275.5 1.3 fusion.23
  276.9 2.6 multiply_convert_fusion.2
  279.5 0.9 pad_maximum_fusion.1
  280.4 7.1 %collective-permute-done.2 = bf16[2,16,32,512]{3,2,1,0:T(8,128)(2,1)} collective-permute-done((bf16[2,16,32,512]{3,2,1,0:T(8,128)(2,1)}, bf16[2,16,32,512]{3,2,1,0:T(8,128)(2,1)}, u32[]{:S(2)}, u32[]{:S(2)}) %collective-permute-start.2) | collective-permute-done | bytes 1048608 | tf_op jit(solution)/shard_map/ppermute | solution.py:52
  287.4 2.4 constant_dynamic-update-slice_fusion.7
  289.8 2.3 constant_dynamic-update-slice_fusion.6
  292.2 2.4 constant_dynamic-update-slice_fusion.5
  294.6 0.0 copy-done
  294.6 1.2 constant_dynamic-update-slice_fusion.4
  295.8 2.3 constant_dynamic-update-slice_fusion.3
  298.1 2.3 constant_dynamic-update-slice_fusion.2
  300.4 0.0 copy-done.3
  300.4 1.1 constant_dynamic-update-slice_fusion.1
  301.5 1.2 constant_dynamic-update-slice_fusion
  302.8 0.0 all-to-all-done
  302.8 382.5 %conditional.1 = (bf16[256,128,201]{1,0,2:T(8,128)(2,1)}) conditional(s32[]{:T(128)} %convert_element_type.36, () %tuple.22, (s32[]{:T(128)}, s32[]{:T(128)}, bf16[2,16,256,512]{3,2,1,0:T(8,128)(2,1)}, bf16[2,16,1,2,4,32,512]{6,5,3,1,0,4,2:T(8,128)(2,1)}, bf16[1024,201]{1,0:T(8,128)(2,1)}, /*index=5*/s32[]{:T(128)}, s32[]{:T(128)}) %tuple.29), branch_computations={%region_1.2_spmd, %region_2.3_spmd.clone} | conditional | flops 15750201344 | bytes 815425728 | solution.py:71
  302.8 14.5 %copy.21 = bf16[2,16,256,512]{2,1,3,0:T(8,128)(2,1)} copy(bf16[2,16,256,512]{3,2,1,0:T(8,128)(2,1)} %get-tuple-element.129) | data formatting | bytes 16777216 | tf_op jit(solution)/shard_map
  317.3 6.1 fusion.25
  323.3 7.9 %copy.15 = bf16[16,256,512]{1,0,2:T(8,128)(2,1)} copy(bf16[16,256,512]{2,1,0:T(8,128)(2,1)} %bitcast.57) | data formatting | bytes 8388608 | tf_op jit(solution)/shard_map/cond/branch_1_fun/squeeze | solution.py:35
  331.3 7.9 %copy.16 = bf16[16,256,512]{1,0,2:T(8,128)(2,1)} copy(bf16[16,256,512]{2,1,0:T(8,128)(2,1)} %bitcast.56) | data formatting | bytes 8388608 | tf_op jit(solution)/shard_map/cond/branch_1_fun/squeeze | solution.py:36
  339.2 27.3 %fusion.11 = f32[512,128,256]{2,1,0:T(8,128)} fusion(bf16[16,256,512]{1,0,2:T(8,128)(2,1)} %copy.16, bf16[2,16,256,512]{2,1,3,0:T(8,128)(2,1)} %copy.21, s32[]{:T(128)S(6)} %select_n.30), kind=kOutput, calls=%fused_computation.13 | convolution fusion | flops 536870912 | bytes 73400320 | tf_op jit(solution)/shard_map/cond/branch_1_fun/wap,wbp->abp/dot_general | solution.py:37
  366.5 37.7 %fusion.10 = bf16[256,128,1,512]{0,1,3,2:T(8,128)(2,1)} fusion(f32[512,128,256]{2,1,0:T(8,128)} %fusion.11, bf16[16,256,512]{1,0,2:T(8,128)(2,1)} %copy.15, bf16[2,16,256,512]{2,1,3,0:T(8,128)(2,1)} %copy.21, s32[]{:T(128)S(6)} %add.77, s32[]{:T(128)S(6)} %select_n.30), kind=kOutput, calls=%fused_computation.9 | convolution fusion | flops 570425344 | bytes 106954760 | tf_op jit(solution)/shard_map/cond/branch_1_fun/wap,wbp->abp/dot_general | solution.py:39
  404.2 27.3 %fusion.12 = f32[512,128,256]{2,1,0:T(8,128)} fusion(bf16[16,256,512]{1,0,2:T(8,128)(2,1)} %copy.15, bf16[2,16,256,512]{2,1,3,0:T(8,128)(2,1)} %copy.21, s32[]{:T(128)S(6)} %select_n.30), kind=kOutput, calls=%fused_computation.14 | convolution fusion | flops 536870912 | bytes 73400320 | tf_op jit(solution)/shard_map/cond/branch_1_fun/wap,wbp->abp/dot_general | solution.py:34
  431.5 37.7 %fusion.9 = bf16[256,128,1,512]{0,1,3,2:T(8,128)(2,1)} fusion(f32[512,128,256]{2,1,0:T(8,128)} %fusion.12, bf16[16,256,512]{1,0,2:T(8,128)(2,1)} %copy.16, bf16[2,16,256,512]{2,1,3,0:T(8,128)(2,1)} %copy.21, s32[]{:T(128)S(6)} %add.77, s32[]{:T(128)S(6)} %select_n.30), kind=kOutput, calls=%fused_computation.8 | convolution fusion | flops 570425344 | bytes 106954760 | tf_op jit(solution)/shard_map/cond/branch_1_fun/wap,wbp->abp/dot_general | solution.py:36
  469.2 44.7 %pad_maximum_fusion = bf16[256,128,2,512]{0,1,3,2:T(8,128)(2,1)} fusion(bf16[256,128,1,512]{0,1,3,2:T(8,128)(2,1)} %fusion.10, bf16[256,128,1,512]{0,1,3,2:T(8,128)(2,1)} %fusion.9), kind=kLoop, calls=%fused_computation.3 | loop fusion | flops 33554432 | bytes 134217728 | tf_op jit(solution)/shard_map/cond/branch_1_fun/stack | solution.py:40
  513.9 0.0 copy-start.4
  513.9 81.4 %copy.19 = bf16[256,128,2,512]{1,0,3,2:T(8,128)(2,1)} copy(bf16[256,128,2,512]{0,1,3,2:T(8,128)(2,1)} %pad_maximum_fusion) | data formatting | bytes 134217728 | tf_op jit(solution)/shard_map/cond/branch_1_fun/stack | solution.py:40
  595.3 0.0 copy-done.4
  595.3 75.6 %fusion.6 = bf16[32768,201]{0,1:T(8,128)(2,1)} fusion(bf16[1024,201]{1,0:T(8,128)(2,1)S(1)} %copy-done.4, bf16[128,8,256,128]{3,2,1,0:T(8,128)(2,1)} %bitcast.19), kind=kOutput, calls=%fused_computation.7 | convolution fusion | flops 13502054400 | bytes 80693248 | tf_op jit(solution)/shard_map/cond/branch_1_fun/dot_general | solution.py:44
  670.9 8.4 %copy.24 = bf16[26,8,256,128]{3,2,1,0:T(8,128)(2,1)S(1)} copy(bf16[26,8,256,128]{3,1,2,0:T(8,128)(2,1)} %bitcast.58) | data formatting | bytes 27262976 | tf_op jit(solution)/shard_map/cond
  679.3 6.0 slice_bitcast_fusion
  (3 shorter events, 0.0 us)
Async XLA Ops:
  6.5 132.4 %all-gather.2.cloned.1.call-start = ((), (), s32[]{:S(2)}) async-start(), calls=%async_computation.1 | async-start | bytes 9437184 | tf_op jit(solution)/shard_map/all_gather | solution.py:64
  147.4 5.9 copy-start.1
  147.4 126.2 %copy-start.5 = (s32[2]{0:T(128)S(1)}, s32[2]{0:T(128)}, u32[]{:S(2)}) copy-start(s32[2]{0:T(128)} %param.7) | copy-start | bytes 28
  147.4 147.2 %copy-start = (f32[2,16,32,512]{3,2,1,0:T(8,128)S(1)}, f32[2,16,32,512]{3,2,1,0:T(8,128)}, u32[]{:S(2)}) copy-start(f32[2,16,32,512]{3,2,1,0:T(8,128)} %param.5) | copy-start | bytes 6291460
  147.4 155.4 %all-to-all-start = ((bf16[2,16,4,2,32,512]{5,4,3,1,0,2:T(8,128)(2,1)}), bf16[2,16,4,2,32,512]{5,4,3,1,0,2:T(8,128)(2,1)}, u32[]{:S(2)}, u32[]{:S(2)}) async-start(bf16[2,16,4,2,32,512]{5,4,3,1,0,2:T(8,128)(2,1)} %copy.20), calls=%async_computation | async-start | bytes 16777216 | tf_op jit(solution)/shard_map/all_to_all | solution.py:66
  153.3 104.3 %collective-permute-start = (bf16[2,16,32,512]{3,2,1,0:T(8,128)(2,1)S(1)}, bf16[2,16,32,512]{3,2,1,0:T(8,128)(2,1)S(1)}, u32[]{:S(2)}, u32[]{:S(2)}) collective-permute-start(bf16[2,16,32,512]{3,2,1,0:T(8,128)(2,1)S(1)} %copy-done.1), channel_id=1, source_target_pairs={{0,8},{8,16},{16,24},{24,0},{1,9},{9,17},{17,25},{25,1},{2,10},{10... | collective-permute-start | bytes 3145736 | tf_op jit(solution)/shard_map/ppermute | solution.py:52
  257.6 1.0 copy-start.2
  258.6 14.3 %collective-permute-start.1 = (bf16[2,16,32,512]{3,2,1,0:T(8,128)(2,1)S(1)}, bf16[2,16,32,512]{3,2,1,0:T(8,128)(2,1)}, u32[]{:S(2)}, u32[]{:S(2)}) collective-permute-start(bf16[2,16,32,512]{3,2,1,0:T(8,128)(2,1)S(1)} %collective-permute-done), channel_id=1, source_target_pairs={{0,8},{8,16},{16,24},{24,0},{1,9},{9,17},{17,25},{25,1},{2,10},{10... | collective-permute-start | bytes 3145736 | tf_op jit(solution)/shard_map/ppermute | solution.py:52
  258.6 41.9 %copy-start.3 = (bf16[2,16,32,512]{3,2,1,0:T(8,128)(2,1)S(1)}, bf16[2,16,32,512]{3,2,1,0:T(8,128)(2,1)}, u32[]{:S(2)}) copy-start(bf16[2,16,32,512]{3,2,1,0:T(8,128)(2,1)} %copy-done.2) | copy-start | bytes 3145732
  272.9 14.5 %collective-permute-start.2 = (bf16[2,16,32,512]{3,2,1,0:T(8,128)(2,1)}, bf16[2,16,32,512]{3,2,1,0:T(8,128)(2,1)}, u32[]{:S(2)}, u32[]{:S(2)}) collective-permute-start(bf16[2,16,32,512]{3,2,1,0:T(8,128)(2,1)} %collective-permute-done.1), channel_id=1, source_target_pairs={{0,8},{8,16},{16,24},{24,0},{1,9},{9,17},{17,25},{25,1},{2,10},{10... | collective-permute-start | bytes 3145736 | tf_op jit(solution)/shard_map/ppermute | solution.py:52
  513.9 81.4 %copy-start.4 = (bf16[1024,201]{1,0:T(8,128)(2,1)S(1)}, bf16[1024,201]{1,0:T(8,128)(2,1)}, u32[]{:S(2)}) copy-start(bf16[1024,201]{1,0:T(8,128)(2,1)} %get-tuple-element.109) | copy-start | bytes 1234948 | tf_op jit(solution)/shard_map/cond
Sparse Core Ops, SparseCore 0:
  11.3 127.5 all-gather.1
